TPU v7x, 32 devices: a whole 2x2x4 slice. The times are simulated.
32 devices in a mesh: dp: 2 (over core), seqo: 4 (over y, x), seqi: 4 (over z).
Axes of the slice: x: 2, y: 2, z: 4, core: 2. Of those that a mesh axis runs over, the one named last changes fastest.
Arguments:
- loaded: bfloat16 [4096, 1024], P(('dp', 'seqo', 'seqi')), parts along dimension 0, may hold values from -6 to 6
- packing: int32 [8, 4, 4, 2], P(('dp', 'seqo')), parts along dimension 0, may hold values from 0 to 128, as said below
- pattern: int32 [32, 64, 64], P(('dp', 'seqo', 'seqi')), parts along dimension 0, may hold values from 0 to 1, as said below
- w_query: bfloat16 [1024, 1024], replicated, may hold values from -0.1875 to 0.1875
- w_key: bfloat16 [1024, 1024], replicated, may hold values from -0.1875 to 0.1875
- w_value: bfloat16 [1024, 1024], replicated, may hold values from -0.1875 to 0.1875
- norm_gain: float32 [1024], replicated, may hold values from 0.25 to 1.75
- w_out: bfloat16 [1024, 1024], replicated, may hold values from -0.1875 to 0.1875
Outputs:
- mixed: float32 [4096, 1024], P(('dp', 'seqo', 'seqi')), parts along dimension 0
There are 2 independent parts, one for each index of `dp`. A program takes and returns all parts, laid end to end along the dimension named above; an argument that names none is the same for every part. Nothing has to cross between parts.
Inputs may be any that keep to these rules, and one draw needn't show every extreme that they name: `packing`: for each group and source s the counts over d sum to 128 and the offsets are their running sums in the order of d; for each destination d the counts over s sum to 128; a count is at most 64, and some count of every group equals 64. pattern[c, i, j] is 1 where j == i and 0 where j > i.
All inputs are finite; a program needn't handle non-finite values.
Results may differ from a plain program's by a relative error of at most 0.0053.
Values may be sent and summed in bfloat16 or wider, within the bound.
No kernel may reach another device: no remote copies, remote signals or barrier semaphores. Data moves between devices by JAX's collectives and lax.ppermute only.
A program may use at most 128 MiB of HBM per device.

v0:
```python
import jax
import jax.numpy as jnp
from jax import lax
from jax.sharding import PartitionSpec as P

H = 16
NB = 64
EPSILON = 1e-06


def prefix_2(value, axis, join, neutral):
    count, mine = (lax.axis_size(axis), lax.axis_index(axis))
    pieces = lax.all_gather(value, axis)
    so_far = jnp.full_like(value, 0) + jnp.asarray(neutral, value.dtype)

    def turn(position, so_far):
        longer = join(so_far, pieces[position])
        return jnp.where(position < mine, longer, so_far)

    return lax.fori_loop(0, count - 1, turn, so_far)


def add_states(earlier, later):
    return earlier + later


def project_columns(rows, w_query, w_key, w_value):
    return tuple(
        (
            jnp.einsum("td,de->et", rows, weight, preferred_element_type=jnp.float32).astype(
                jnp.bfloat16
            )
            for weight in (w_query, w_key, w_value)
        )
    )


def body(loaded, packing, pattern, w_query, w_key, w_value, norm_gain, w_out):
    sources = lax.axis_size("seqi")
    rows_dev = loaded.shape[0]
    feature_width = loaded.shape[1]
    capacity = 2 * rows_dev // sources
    my_index = lax.axis_index("seqi")
    source_ids = jnp.arange(sources, dtype=jnp.int32)
    select = (source_ids == my_index).astype(jnp.int32)
    table = packing[0]
    outgoing = jnp.sum(table * select[:, None, None], axis=0)
    slot_ids = jnp.arange(capacity, dtype=jnp.int32)
    valid = slot_ids[None, :] < outgoing[:, 1:2]
    slot_rows = jnp.where(valid, outgoing[:, 0:1] + slot_ids[None, :], 0)
    slots = jnp.take(loaded, slot_rows.reshape(-1), axis=0).reshape(
        sources, capacity, feature_width
    )
    slots = jnp.where(valid[:, :, None], slots, jnp.zeros((), jnp.bfloat16))
    incoming = jnp.sum(table[:, :, 1] * select[None, :], axis=1)
    ends = jnp.cumsum(incoming)
    starts = ends - incoming
    row_ids = jnp.arange(rows_dev, dtype=jnp.int32)
    source_of = jnp.sum((row_ids[:, None] >= ends[None, :]).astype(jnp.int32), axis=1)
    picked = (source_of[:, None] == source_ids[None, :]).astype(jnp.int32)
    first_row = jnp.sum(picked * starts[None, :], axis=1)
    unpack = source_of * capacity + row_ids - first_row
    arrived = lax.all_to_all(slots, "seqi", split_axis=0, concat_axis=0, tiled=True)
    tokens = jnp.take(arrived.reshape(sources * capacity, feature_width), unpack, axis=0)
    query_cols, key_cols, value_cols = project_columns(tokens, w_query, w_key, w_value)
    head_size = feature_width // H
    query_heads = query_cols.reshape(H, head_size, rows_dev)
    key_heads = key_cols.reshape(H, head_size, rows_dev)
    value_heads = value_cols.reshape(H, head_size, rows_dev)
    state = jnp.einsum("hdt,het->hde", key_heads, value_heads, preferred_element_type=jnp.float32)
    zero_state = jnp.zeros_like(state)
    inner = prefix_2(state, "seqi", add_states, zero_state)
    group_sum = lax.psum(state, "seqi")
    outer = prefix_2(group_sum, "seqo", add_states, zero_state)
    prefix = outer + inner
    scores = jnp.einsum("hdt,hds->hts", query_heads, key_heads, preferred_element_type=jnp.float32)
    frames = jnp.arange(rows_dev, dtype=jnp.int32) // (rows_dev // NB)
    allowed = pattern[0][frames][:, frames] > 0
    masked = jnp.where(allowed[None], scores, jnp.zeros((), jnp.float32)).astype(jnp.bfloat16)
    local = jnp.einsum("hts,hes->het", masked, value_heads, preferred_element_type=jnp.float32)
    carried = jnp.einsum(
        "hdt,hde->het", query_heads.astype(jnp.float32), prefix, precision=lax.Precision.HIGHEST
    )
    attended = local + carried
    factor = lax.rsqrt(jnp.mean(attended * attended, axis=1, keepdims=True) + EPSILON)
    gain = norm_gain.reshape(H, head_size, 1)
    normed = (attended * factor * gain).astype(jnp.bfloat16).reshape(feature_width, rows_dev)
    return jnp.einsum("dt,de->te", normed, w_out, preferred_element_type=jnp.float32)


def solution(mesh):
    return jax.shard_map(
        body,
        mesh=mesh,
        in_specs=(
            P(("dp", "seqo", "seqi"), None),
            P(("dp", "seqo"), None, None, None),
            P(("dp", "seqo", "seqi"), None, None),
            P(),
            P(),
            P(),
            P(),
            P(),
        ),
        out_specs=P(("dp", "seqo", "seqi"), None),
        check_vma=False,
    )
```

profile of v0, /device:TPU:0, one launch (start us, length us, event | category | flops | bytes accessed | tf_op | source)
XLA Modules:
  0.0 176.0 jit_solution(17563134460759956328)
XLA Ops:
  6.5 0.9 multiply_reduce_fusion.1
  7.7 2.5 %gather_fusion = bf16[256,1024]{1,0:T(8,128)(2,1)S(1)} fusion(bf16[128,1024]{1,0:T(8,128)(2,1)} %param.12, s32[1024]{0:T(1024)S(1)} %pad_clamp_fusion.2), kind=kCustom, calls=%fused_computation | custom fusion | bytes 1049600 | tf_op jit(solution)/shard_map/jit(_take)/gather | solution.py:51
  10.3 0.9 select_select_fusion
  11.2 6.3 %all-to-all-start = ((bf16[4,64,1024]{2,1,0:T(8,128)(2,1)}), bf16[4,64,1024]{2,1,0:T(8,128)(2,1)S(1)}, u32[]{:S(2)}, u32[]{:S(2)}) async-start(bf16[4,64,1024]{2,1,0:T(8,128)(2,1)} %select_select_fusion), calls=%async_computation | async-start | bytes 1048576 | tf_op jit(solution)/shard_map/all_to_all | solution.py:63
  17.7 0.2 reduce-window.7
  18.1 14.0 %all-to-all-done = bf16[4,64,1024]{2,1,0:T(8,128)(2,1)S(1)} async-done(((bf16[4,64,1024]{2,1,0:T(8,128)(2,1)}), bf16[4,64,1024]{2,1,0:T(8,128)(2,1)S(1)}, u32[]{:S(2)}, u32[]{:S(2)}) %all-to-all-start) | async-done | bytes 524320 | tf_op jit(solution)/shard_map/all_to_all | solution.py:63
  32.1 0.9 gather_fusion.1
  32.9 0.5 fusion.3
  33.4 0.2 copy.32
  33.6 2.2 %fusion.5 = bf16[1024,128]{0,1:T(8,128)(2,1)S(1)} fusion(bf16[1024,1024]{1,0:T(8,128)(2,1)} %param.16, bf16[128,1024]{1,0:T(8,128)(2,1)S(1)} %gather_fusion.1, pred[128]{0:T(512)(128)(4,1)S(1)} %compare_and_fusion.1), kind=kOutput, calls=%fused_computation.15 | convolution fusion | flops 268697600 | bytes 2621568 | tf_op jit(solution)/shard_map/td,de->et/dot_general | solution.py:30
  35.8 0.2 copy.36
  36.0 1.1 fusion.15
  37.1 44.9 %all-gather.6.cloned.1.call-done = f32[64,64,64]{2,1,0:T(8,128)} async-done(((f32[16,64,64]{2,1,0:T(8,128)}), f32[64,64,64]{2,1,0:T(8,128)}) %all-gather.6.cloned.1.call-update) | async-done | bytes 1048592 | tf_op jit(solution)/shard_map/all_gather | solution.py:13
  82.0 0.7 all-reduce.2.cloned.1.call-update
  82.8 39.7 %all-reduce.2.cloned.1.call-done = f32[1,16,64,64]{3,2,1,0:T(8,128)} async-done(((f32[1,16,64,64]{3,2,1,0:T(8,128)}), f32[1,16,64,64]{3,2,1,0:T(8,128)}) %all-reduce.2.cloned.1.call-update) | async-done | bytes 262160 | tf_op jit(solution)/shard_map/psum | solution.py:73
  122.6 0.6 gather_fusion.2
  123.3 0.7 gather_fusion.3
  124.2 2.8 %fusion.4 = bf16[1024,128]{0,1:T(8,128)(2,1)} fusion(bf16[1024,1024]{1,0:T(8,128)(2,1)} %param.15, bf16[128,1024]{1,0:T(8,128)(2,1)S(1)} %gather_fusion.1, pred[128]{0:T(512)(128)(4,1)S(1)} %compare_and_fusion.1), kind=kOutput, calls=%fused_computation.14 | convolution fusion | flops 268697600 | bytes 2621568 | tf_op jit(solution)/shard_map/td,de->et/dot_general | solution.py:30
  127.0 1.1 copy.35
  128.1 3.8 %while.29 = (s32[]{:T(128)}, f32[16,64,64]{2,1,0:T(8,128)S(1)}, s32[]{:T(128)}, f32[4,16,64,64]{3,2,1,0:T(8,128)}, s32[]{:T(128)}, /*index=5*/s32[]{:T(128)}) while((s32[]{:T(128)}, f32[16,64,64]{2,1,0:T(8,128)S(1)}, s32[]{:T(128)}, f32[4,16,64,64]{3,2,1,0:T(8,128)}, s32[]{:T(128)}, /*index=5*/s32[]{:T(128)}) %tuple.74), condition=%wide.region_9.10_spmd.clone, body=%wide.region_8.9_spmd.clone.sunk | while | flops 196612 | bytes 786525 | solution.py:20
  128.1 1.2 add_select_fusion.6
  129.4 1.2 add_select_fusion.6
  130.6 1.3 add_select_fusion.6
  131.9 27.5 %all-gather.4.cloned.1.call-done = f32[4,16,64,64]{3,2,1,0:T(8,128)} async-done(((f32[1,16,64,64]{3,2,1,0:T(8,128)}), f32[4,16,64,64]{3,2,1,0:T(8,128)}) %all-gather.4.cloned.1.call-update) | async-done | bytes 1048592 | tf_op jit(solution)/shard_map/all_gather | solution.py:13
  159.4 3.7 %while.28 = (s32[]{:T(128)}, f32[16,64,64]{2,1,0:T(8,128)S(1)}, s32[]{:T(128)}, f32[4,16,64,64]{3,2,1,0:T(8,128)}, s32[]{:T(128)}, /*index=5*/s32[]{:T(128)}) while((s32[]{:T(128)}, f32[16,64,64]{2,1,0:T(8,128)S(1)}, s32[]{:T(128)}, f32[4,16,64,64]{3,2,1,0:T(8,128)}, s32[]{:T(128)}, /*index=5*/s32[]{:T(128)}) %tuple.62), condition=%wide.region_7.8_spmd.clone, body=%wide.region_6.7_spmd.clone.sunk | while | flops 196612 | bytes 786525 | solution.py:20
  159.4 1.2 add_select_fusion.5
  160.6 1.2 add_select_fusion.5
  161.9 1.2 add_select_fusion.5
  163.1 1.4 fusion.6
  164.5 1.9 %multiply_reduce_fusion = (f32[16,128]{1,0:T(8,128)S(1)}, f32[16,64,128]{2,1,0:T(8,128)S(1)}) fusion(f32[16,64,128]{2,1,0:T(8,128)} %fusion.6, bf16[16,64,128]{2,1,0:T(8,128)(2,1)} %bitcast.74, bf16[16,64,128]{2,1,0:T(8,128)(2,1)S(1)} %bitcast.72, bf16[16,64,128]{2,1,0:T(8,128)(2,1)} %bitcast.76, pred[128,128]{1,0:T(8,128)(4,1)S(1)} %copy.34), kind=kOutput, calls=%fused_computation.17 | convolution fusion | flops 68024320 | bytes 1859584 | tf_op jit(solution)/shard_map/hts,hes->het/dot_general | solution.py:80
  166.4 0.2 multiply_convert_fusion
  166.6 2.9 %fusion.16 = f32[128,1024]{1,0:T(8,128)} fusion(bf16[1024,128]{1,0:T(8,128)(2,1)S(1)} %bitcast.78, bf16[1024,1024]{1,0:T(8,128)(2,1)} %param.19), kind=kOutput, calls=%fused_computation.61 | convolution fusion | flops 268435456 | bytes 2883584 | tf_op jit(solution)/shard_map/dt,de->te/dot_general | solution.py:88
  (41 shorter events, 1.0 us)
Async XLA Ops:
  6.5 26.4 %copy-start = (bf16[1024,1024]{1,0:T(8,128)(2,1)S(1)}, bf16[1024,1024]{1,0:T(8,128)(2,1)}, u32[]{:S(2)}) copy-start(bf16[1024,1024]{1,0:T(8,128)(2,1)} %param.17) | copy-start | bytes 6291460
  10.3 7.3 %copy-start.4 = (s32[1,4,4,2]{2,3,1,0:T(2,128)S(1)}, s32[1,4,4,2]{2,3,1,0:T(2,128)}, u32[]{:S(2)}) copy-start(s32[1,4,4,2]{2,3,1,0:T(2,128)} %param.13) | copy-start | bytes 388
  11.2 20.8 %all-to-all-start = ((bf16[4,64,1024]{2,1,0:T(8,128)(2,1)}), bf16[4,64,1024]{2,1,0:T(8,128)(2,1)S(1)}, u32[]{:S(2)}, u32[]{:S(2)}) async-start(bf16[4,64,1024]{2,1,0:T(8,128)(2,1)} %select_select_fusion), calls=%async_computation | async-start | bytes 1048576 | tf_op jit(solution)/shard_map/all_to_all | solution.py:63
  17.6 64.4 %all-gather.6.cloned.1.call-start = ((), (), s32[]{:S(2)}) async-start(), calls=%async_computation.3 | async-start | bytes 2621440 | tf_op jit(solution)/shard_map/all_gather | solution.py:13
  33.6 3.5 %copy-start.2 = (bf16[1024,128]{1,0:T(8,128)(2,1)}, bf16[1024,128]{1,0:T(8,128)(2,1)S(1)}, u32[]{:S(2)}) copy-start(bf16[1024,128]{1,0:T(8,128)(2,1)S(1)} %copy.32) | copy-start | bytes 786436
  35.8 86.8 %copy-start.1 = (s32[1,64,64]{2,1,0:T(8,128)S(1)}, s32[1,64,64]{2,1,0:T(8,128)}, u32[]{:S(2)}) copy-start(s32[1,64,64]{2,1,0:T(8,128)} %param.14) | copy-start | bytes 49156
  36.0 86.5 %copy-start.3 = (bf16[1024,128]{1,0:T(8,128)(2,1)}, bf16[1024,128]{1,0:T(8,128)(2,1)S(1)}, u32[]{:S(2)}) copy-start(bf16[1024,128]{1,0:T(8,128)(2,1)S(1)} %copy.36) | copy-start | bytes 786436
  36.0 88.1 %copy-start.5 = (f32[1024]{0:T(1024)S(1)}, f32[1024]{0:T(1024)}, u32[]{:S(2)}) copy-start(f32[1024]{0:T(1024)} %param.18) | copy-start | bytes 12292
  82.0 40.5 %all-reduce.2.cloned.1.call-start = ((), (), s32[]{:S(2)}) async-start(), calls=%async_computation.1 | async-start | bytes 1048576 | tf_op jit(solution)/shard_map/psum | solution.py:73
  82.8 76.6 %all-gather.4.cloned.1.call-start = ((), (), s32[]{:S(2)}) async-start(), calls=%async_computation.2 | async-start | bytes 2621440 | tf_op jit(solution)/shard_map/all_gather | solution.py:13
Sparse Core Ops, SparseCore 0:
  37.2 44.7 all-gather.5
  85.2 37.3 all-reduce.1
  124.4 34.9 all-gather.3
where the time goes:
time: 177 us; the launch traced here: 176 us
  waiting for transfers between devices  127 us (72%)
  between operations  13.3 us (8%)
  matrix products  12.7 us (7%)
  other arithmetic  10.2 us (6%)
  local copies, waits for them, and re-layouts  6.54 us (4%)
  starting transfers between devices  6.39 us (4%)
    all_gather x2, waiting for transfers between devices, prefix_2(): pieces = lax.all_gather(value, axis)  72.4 us
    psum x1, waiting for transfers between devices, body(): group_sum = lax.psum(state, 'seqi')  39.7 us
    all_to_all x1, waiting for transfers between devices, body(): lax.all_to_all(slots, 'seqi', split_axis=0, concat_axis=0, tiled=True)  14 us
    select_n x6, other arithmetic, turn(): return jnp.where(position < mine, longer, so_far)  7.41 us
    all_to_all x1, starting transfers between devices, body(): lax.all_to_all(slots, 'seqi', split_axis=0, concat_axis=0, tiled=True)  6.35 us
    dot_general x3, matrix products, project_columns(): jnp.einsum('td,de->et', rows, weight, preferred_element_type=jnp.float32)  5.45 us
  transfers between devices with their start and end apart: 4, of which 4 were waited for; matrix products, arithmetic and copies ran while one was open for 6% of the time, Pallas kernels for 0%

commit v1 on v0

--- a/solution.py
+++ b/solution.py
@@ -70,7 +70,7 @@
     state = jnp.einsum("hdt,het->hde", key_heads, value_heads, preferred_element_type=jnp.float32)
     zero_state = jnp.zeros_like(state)
     inner = prefix_2(state, "seqi", add_states, zero_state)
-    group_sum = lax.psum(state, "seqi")
+    group_sum = jnp.sum(lax.all_gather(state, "seqi"), axis=0)
     outer = prefix_2(group_sum, "seqo", add_states, zero_state)
     prefix = outer + inner
     scores = jnp.einsum("hdt,hds->hts", query_heads, key_heads, preferred_element_type=jnp.float32)

time: 177 us -> 136 us (0.77)
  waiting for transfers between devices: 127 us -> 83.5 us
  other arithmetic: 10.2 us -> 12.9 us
    all_gather x2 -> x1, waiting for transfers between devices: 72.4 us -> 24.6 us  [prefix_2(): pieces = lax.all_gather(value, axis)]
    all_gather x0 -> x1, waiting for transfers between devices: none -> 44.9 us  [body(): group_sum = jnp.sum(lax.all_gather(state, 'seqi'), axis=0)]
    psum x1 -> x0, waiting for transfers between devices: 39.7 us -> none  [body(): group_sum = lax.psum(state, 'seqi')]
    reduce_sum x0 -> x1, other arithmetic: none -> 2.66 us  [body(): group_sum = jnp.sum(lax.all_gather(state, 'seqi'), axis=0)]
  transfers between devices with their start and end apart: 4 -> 3, of which waited for: 4 -> 3; matrix products, arithmetic and copies ran while one was open for 6% -> 7% of each run, Pallas kernels for 0% -> 0%
where the time goes in v1:
time: 136 us
  waiting for transfers between devices  83.5 us (61%)
  between operations  13.6 us (10%)
  other arithmetic  12.9 us (9%)
  matrix products  12.7 us (9%)
  local copies, waits for them, and re-layouts  6.55 us (5%)
  starting transfers between devices  6.39 us (5%)
    all_gather x1, waiting for transfers between devices, body(): group_sum = jnp.sum(lax.all_gather(state, 'seqi'), axis=0)  44.9 us
    all_gather x1, waiting for transfers between devices, prefix_2(): pieces = lax.all_gather(value, axis)  24.6 us
    all_to_all x1, waiting for transfers between devices, body(): lax.all_to_all(slots, 'seqi', split_axis=0, concat_axis=0, tiled=True)  14 us
    select_n x6, other arithmetic, turn(): return jnp.where(position < mine, longer, so_far)  7.51 us
    all_to_all x1, starting transfers between devices, body(): lax.all_to_all(slots, 'seqi', split_axis=0, concat_axis=0, tiled=True)  6.35 us
    dot_general x3, matrix products, project_columns(): jnp.einsum('td,de->et', rows, weight, preferred_element_type=jnp.float32)  5.46 us
    dot_general x1, matrix products, body(): jnp.einsum('dt,de->te', normed, w_out, preferred_element_type=jnp.float32)  2.86 us
  transfers between devices with their start and end apart: 3, of which 3 were waited for; matrix products, arithmetic and copies ran while one was open for 7% of the time, Pallas kernels for 0%

profile of v1, /device:TPU:0, one launch (start us, length us, event | category | flops | bytes accessed | tf_op | source)
XLA Modules:
  0.0 135.8 jit_solution(4298760954927290589)
XLA Ops:
  6.5 0.9 multiply_reduce_fusion.1
  7.7 2.5 %gather_fusion = bf16[256,1024]{1,0:T(8,128)(2,1)S(1)} fusion(bf16[128,1024]{1,0:T(8,128)(2,1)} %param.12, s32[1024]{0:T(1024)S(1)} %pad_clamp_fusion.2), kind=kCustom, calls=%fused_computation | custom fusion | bytes 1049600 | tf_op jit(solution)/shard_map/jit(_take)/gather | solution.py:51
  10.3 0.9 select_select_fusion
  11.2 6.3 %all-to-all-start = ((bf16[4,64,1024]{2,1,0:T(8,128)(2,1)}), bf16[4,64,1024]{2,1,0:T(8,128)(2,1)S(1)}, u32[]{:S(2)}, u32[]{:S(2)}) async-start(bf16[4,64,1024]{2,1,0:T(8,128)(2,1)} %select_select_fusion), calls=%async_computation | async-start | bytes 1048576 | tf_op jit(solution)/shard_map/all_to_all | solution.py:63
  17.7 0.2 reduce-window.7
  18.1 14.0 %all-to-all-done = bf16[4,64,1024]{2,1,0:T(8,128)(2,1)S(1)} async-done(((bf16[4,64,1024]{2,1,0:T(8,128)(2,1)}), bf16[4,64,1024]{2,1,0:T(8,128)(2,1)S(1)}, u32[]{:S(2)}, u32[]{:S(2)}) %all-to-all-start) | async-done | bytes 524320 | tf_op jit(solution)/shard_map/all_to_all | solution.py:63
  32.1 0.9 gather_fusion.1
  32.9 0.5 fusion.3
  33.4 0.2 copy.32
  33.6 2.2 %fusion.5 = bf16[1024,128]{0,1:T(8,128)(2,1)S(1)} fusion(bf16[1024,1024]{1,0:T(8,128)(2,1)} %param.16, bf16[128,1024]{1,0:T(8,128)(2,1)S(1)} %gather_fusion.1, pred[128]{0:T(512)(128)(4,1)S(1)} %compare_and_fusion.1), kind=kOutput, calls=%fused_computation.15 | convolution fusion | flops 268697600 | bytes 2621568 | tf_op jit(solution)/shard_map/td,de->et/dot_general | solution.py:30
  35.8 0.2 copy.36
  36.0 1.1 fusion.15
  37.1 44.9 %all-gather.5.cloned.1.call-done = f32[64,64,64]{2,1,0:T(8,128)} async-done(((f32[16,64,64]{2,1,0:T(8,128)}), f32[64,64,64]{2,1,0:T(8,128)}) %all-gather.5.cloned.1.call-update) | async-done | bytes 1048592 | tf_op jit(solution)/shard_map/all_gather | solution.py:73
  82.0 2.7 %reduce_sum.61 = f32[16,64,64]{2,1,0:T(8,128)} reduce(f32[4,16,64,64]{3,2,1,0:T(8,128)} %bitcast.68, f32[]{:T(128)} %constant.111.clone.1), dimensions={0}, to_apply=%region_5.6 | reduce | flops 196608 | bytes 1310724 | tf_op jit(solution)/shard_map/reduce_sum | solution.py:73
  84.7 0.6 gather_fusion.2
  85.5 0.7 gather_fusion.3
  86.1 0.1 copy.34
  86.3 2.8 %fusion.4 = bf16[1024,128]{0,1:T(8,128)(2,1)} fusion(bf16[1024,1024]{1,0:T(8,128)(2,1)} %param.15, bf16[128,1024]{1,0:T(8,128)(2,1)S(1)} %gather_fusion.1, pred[128]{0:T(512)(128)(4,1)S(1)} %compare_and_fusion.1), kind=kOutput, calls=%fused_computation.14 | convolution fusion | flops 268697600 | bytes 2621568 | tf_op jit(solution)/shard_map/td,de->et/dot_general | solution.py:30
  89.1 1.1 copy.35
  90.3 3.9 %while.29 = (s32[]{:T(128)}, f32[16,64,64]{2,1,0:T(8,128)S(1)}, s32[]{:T(128)}, f32[4,16,64,64]{3,2,1,0:T(8,128)}, s32[]{:T(128)}, /*index=5*/s32[]{:T(128)}) while((s32[]{:T(128)}, f32[16,64,64]{2,1,0:T(8,128)S(1)}, s32[]{:T(128)}, f32[4,16,64,64]{3,2,1,0:T(8,128)}, s32[]{:T(128)}, /*index=5*/s32[]{:T(128)}) %tuple.72), condition=%wide.region_9.10_spmd.clone, body=%wide.region_8.9_spmd.clone.sunk | while | flops 196612 | bytes 786525 | solution.py:20
  90.3 1.3 add_select_fusion.6
  91.6 1.3 add_select_fusion.6
  92.9 1.2 add_select_fusion.6
  94.2 24.6 %all-gather.7.cloned.1.call-done = f32[64,64,64]{2,1,0:T(8,128)} async-done(((f32[16,64,64]{2,1,0:T(8,128)}), f32[64,64,64]{2,1,0:T(8,128)}) %all-gather.7.cloned.1.call-update) | async-done | bytes 1048592 | tf_op jit(solution)/shard_map/all_gather | solution.py:13
  118.8 3.7 %while.28 = (s32[]{:T(128)}, f32[16,64,64]{2,1,0:T(8,128)S(1)}, s32[]{:T(128)}, f32[4,16,64,64]{3,2,1,0:T(8,128)}, s32[]{:T(128)}, /*index=5*/s32[]{:T(128)}) while((s32[]{:T(128)}, f32[16,64,64]{2,1,0:T(8,128)S(1)}, s32[]{:T(128)}, f32[4,16,64,64]{3,2,1,0:T(8,128)}, s32[]{:T(128)}, /*index=5*/s32[]{:T(128)}) %tuple.73), condition=%wide.region_7.8_spmd.clone, body=%wide.region_6.7_spmd.clone.sunk | while | flops 196612 | bytes 786525 | solution.py:20
  118.8 1.2 add_select_fusion.5
  120.1 1.2 add_select_fusion.5
  121.3 1.2 add_select_fusion.5
  122.6 1.4 %fusion.6 = f32[16,64,128]{2,1,0:T(8,128)} fusion(bf16[16,64,128]{2,1,0:T(8,128)(2,1)S(1)} %bitcast.72, f32[16,64,64]{2,1,0:T(8,128)S(1)} %get-tuple-element.163, f32[16,64,64]{2,1,0:T(8,128)S(1)} %get-tuple-element.164), kind=kOutput, calls=%fused_computation.18 | convolution fusion | flops 100728832 | bytes 1310720 | tf_op jit(solution)/shard_map/hdt,hde->het/dot_general | solution.py:81
  124.0 1.9 %multiply_reduce_fusion = (f32[16,128]{1,0:T(8,128)S(1)}, f32[16,64,128]{2,1,0:T(8,128)S(1)}) fusion(f32[16,64,128]{2,1,0:T(8,128)} %fusion.6, bf16[16,64,128]{2,1,0:T(8,128)(2,1)} %bitcast.75, bf16[16,64,128]{2,1,0:T(8,128)(2,1)S(1)} %bitcast.73, bf16[16,64,128]{2,1,0:T(8,128)(2,1)} %bitcast.77, pred[128,128]{1,0:T(8,128)(4,1)S(1)} %copy.34), kind=kOutput, calls=%fused_computation.17 | convolution fusion | flops 68024320 | bytes 1859584 | tf_op jit(solution)/shard_map/hts,hes->het/dot_general | solution.py:80
  125.9 0.2 multiply_convert_fusion
  126.1 2.9 %fusion.16 = f32[128,1024]{1,0:T(8,128)} fusion(bf16[1024,128]{1,0:T(8,128)(2,1)S(1)} %bitcast.79, bf16[1024,1024]{1,0:T(8,128)(2,1)} %param.19), kind=kOutput, calls=%fused_computation.61 | convolution fusion | flops 268435456 | bytes 2883584 | tf_op jit(solution)/shard_map/dt,de->te/dot_general | solution.py:88
  (39 shorter events, 0.9 us)
Async XLA Ops:
  6.5 26.4 %copy-start = (bf16[1024,1024]{1,0:T(8,128)(2,1)S(1)}, bf16[1024,1024]{1,0:T(8,128)(2,1)}, u32[]{:S(2)}) copy-start(bf16[1024,1024]{1,0:T(8,128)(2,1)} %param.17) | copy-start | bytes 6291460
  10.3 7.3 %copy-start.4 = (s32[1,4,4,2]{2,3,1,0:T(2,128)S(1)}, s32[1,4,4,2]{2,3,1,0:T(2,128)}, u32[]{:S(2)}) copy-start(s32[1,4,4,2]{2,3,1,0:T(2,128)} %param.13) | copy-start | bytes 388
  11.2 20.8 %all-to-all-start = ((bf16[4,64,1024]{2,1,0:T(8,128)(2,1)}), bf16[4,64,1024]{2,1,0:T(8,128)(2,1)S(1)}, u32[]{:S(2)}, u32[]{:S(2)}) async-start(bf16[4,64,1024]{2,1,0:T(8,128)(2,1)} %select_select_fusion), calls=%async_computation | async-start | bytes 1048576 | tf_op jit(solution)/shard_map/all_to_all | solution.py:63
  17.6 64.4 %all-gather.5.cloned.1.call-start = ((), (), s32[]{:S(2)}) async-start(), calls=%async_computation.1 | async-start | bytes 2621440 | tf_op jit(solution)/shard_map/all_gather | solution.py:73
  33.6 3.4 %copy-start.2 = (bf16[1024,128]{1,0:T(8,128)(2,1)}, bf16[1024,128]{1,0:T(8,128)(2,1)S(1)}, u32[]{:S(2)}) copy-start(bf16[1024,128]{1,0:T(8,128)(2,1)S(1)} %copy.32) | copy-start | bytes 786436
  36.0 48.7 %copy-start.3 = (bf16[1024,128]{1,0:T(8,128)(2,1)}, bf16[1024,128]{1,0:T(8,128)(2,1)S(1)}, u32[]{:S(2)}) copy-start(bf16[1024,128]{1,0:T(8,128)(2,1)S(1)} %copy.36) | copy-start | bytes 786436
  37.0 47.7 %copy-start.1 = (s32[1,64,64]{2,1,0:T(8,128)S(1)}, s32[1,64,64]{2,1,0:T(8,128)}, u32[]{:S(2)}) copy-start(s32[1,64,64]{2,1,0:T(8,128)} %param.14) | copy-start | bytes 49156
  37.1 81.8 %all-gather.7.cloned.1.call-start = ((), (), s32[]{:S(2)}) async-start(), calls=%async_computation.2 | async-start | bytes 2621440 | tf_op jit(solution)/shard_map/all_gather | solution.py:13
  82.0 4.3 %copy-start.5 = (f32[1024]{0:T(1024)S(1)}, f32[1024]{0:T(1024)}, u32[]{:S(2)}) copy-start(f32[1024]{0:T(1024)} %param.18) | copy-start | bytes 12292
Sparse Core Ops, SparseCore 0:
  37.2 44.7 all-gather.4
  84.8 33.9 all-gather.6
